TPU v7x, 128 devices: a whole 4x4x4 slice. The times are simulated.
128 devices in a mesh: dp: 16 (over x, y_hi, core), mp: 8 (over y_lo, z).
Axes of the slice: x: 4, y: 4 (y_hi: 2, y_lo: 2; y = y_hi * 2 + y_lo), z: 4, core: 2. Of those that a mesh axis runs over, the one named last changes fastest.
Arguments:
- hidden: bfloat16 [16384, 2048], P(('dp', 'mp')), may hold values from -4 to 4
- norm_gains: float32 [3, 2048], replicated, may hold values from 0.5 to 1.5
- head_gains: float32 [3, 128], replicated, may hold values from 0.25 to 1.75
- query_weight: bfloat16 [2048, 2048], P(('dp', 'mp')), may hold values from -0.125 to 0.125
- kv_weight: bfloat16 [2048, 512], P(('dp', 'mp')), may hold values from -0.125 to 0.125
- out_weight: bfloat16 [2048, 2048], P(('dp', 'mp')), may hold values from -0.5 to 0.5
- gate_up: bfloat16 [128, 2048, 1536], P(('dp', 'mp')), may hold values from -0.125 to 0.125
- down_weight: bfloat16 [128, 768, 2048], P(('dp', 'mp')), may hold values from -0.21875 to 0.21875
- next_weight: bfloat16 [2048, 512], P(('dp', 'mp')), may hold values from -0.125 to 0.125
- expert_ids: int32 [16384, 8], P(('dp', 'mp')), may hold values from 0 to 127, all different within a row; in each aligned block of 128 rows (0 to 127, 128 to 255, ...) at most 10 rows name the same one
- route_weights: float32 [16384, 8], P(('dp', 'mp')), may hold values from 0.05 to 0.5
- token_request: int32 [16384], P('dp'), may hold values from 0 to 31, as said below
- request_leaf: int32 [32], replicated, may hold values from 0 to 15
- leaf_parent: int32 [16], replicated, may hold values from 0 to 7
- mid_parent: int32 [8], replicated, may hold values from 0 to 7
- root_length: int32 [8], replicated, may hold values from 1 to 512, as said below
- mid_length: int32 [8], replicated, may hold values from 1 to 256, as said below
- leaf_length: int32 [16], replicated, may hold values from 1 to 128, as said below
- root_slot: int32 [8], replicated, may hold values from 0 to 7, each once
- mid_slot: int32 [8], replicated, may hold values from 0 to 7, each once
- leaf_slot: int32 [16], replicated, may hold values from 0 to 15, each once
- root_cache: bfloat16 [8, 512, 512], P('mp'), may hold values from -300 to 300
- mid_cache: bfloat16 [8, 256, 512], P('mp'), may hold values from -300 to 300
- leaf_cache: bfloat16 [16, 128, 512], P('mp'), may hold values from -300 to 300
Outputs:
- layer_out: bfloat16 [16384, 2048], P(('dp', 'mp'))
- next_rows: bfloat16 [16384, 512], P(('dp', 'mp'))
Inputs may be any that keep to these rules, and one draw needn't show every extreme that they name: `expert_ids`: each row names 8 different experts; among the rows of one device no expert is named more than 10 times, a bound that some block reaches. `token_request`: Nondecreasing; tokens g * 1024 to (g + 1) * 1024 - 1 belong to requests g * 2 to (g + 1) * 2 - 1, and every request has at least one token. `root_length`: some root node has the full length. `mid_length`: some middle node has the full length. `leaf_length`: some leaf node has the full length. `root_slot`: each slot once; slot s is on index s // 1 of mp. `mid_slot`: each slot once; slot s is on index s // 1 of mp. `leaf_slot`: each slot once; slot s is on index s // 2 of mp.
All inputs are finite; a program needn't handle non-finite values.
Results may differ from a plain program's by a relative error of at most 0.024.
Values may be sent and summed in bfloat16 or wider, within the bound.
No kernel may reach another device: no remote copies, remote signals or barrier semaphores. Data moves between devices by JAX's collectives and lax.ppermute only.
A program may use at most 192 MiB of HBM per device.

v0:
```python
import jax
import jax.numpy as jnp
from jax import lax
from jax.sharding import PartitionSpec as P

REQ_GRP = 2
EPS = 1e-06
THETA = 1000000.0
MASKED = -1e30


def rms_norm(values, weight_row):
    values = values.astype(jnp.float32)
    return values * lax.rsqrt(jnp.mean(values * values, axis=-1, keepdims=True) + EPS) * weight_row


def rotate(values, positions):
    half_dim = values.shape[-1] // 2
    frequency = THETA ** (-2.0 * jnp.arange(half_dim, dtype=jnp.float32) / values.shape[-1])
    angles = positions.astype(jnp.float32)[:, None] * frequency[None, :]
    cosine = jnp.cos(angles)[:, None, :]
    sine_part = jnp.sin(angles)[:, None, :]
    front_part = values[..., :half_dim]
    back_part = values[..., half_dim:]
    return jnp.concatenate(
        [front_part * cosine - back_part * sine_part, back_part * cosine + front_part * sine_part],
        axis=-1,
    )


def look_up(lookup_table, indices):
    places = jnp.arange(lookup_table.shape[0], dtype=jnp.int32)
    return jnp.sum(jnp.where(indices[:, None] == places[None, :], lookup_table[None, :], 0), axis=1)


def tree_paths(requests, request_leaf, leaf_parent, mid_parent, lengths, slot_tables):
    leaf_node = look_up(request_leaf, requests)
    mid_node = look_up(leaf_parent, leaf_node)
    root_node = look_up(mid_parent, mid_node)
    node_sets = (root_node, mid_node, leaf_node)
    path_slots = [
        look_up(slot_table, node_ids) for slot_table, node_ids in zip(slot_tables, node_sets)
    ]
    path_lengths = [
        look_up(length_table, node_ids) for length_table, node_ids in zip(lengths, node_sets)
    ]
    return (path_slots, path_lengths)


def head_scores(queries, key_rows, allowed):
    kv_heads = queries.shape[1]
    head_dim = queries.shape[3]
    score_scale = head_dim ** (-0.5)
    outcome = []
    for head_no in range(kv_heads):
        key_part = key_rows[:, head_no * head_dim : (head_no + 1) * head_dim]
        raw_scores = (
            jnp.einsum(
                "ngd,pd->ngp", queries[:, head_no], key_part, preferred_element_type=jnp.float32
            )
            * score_scale
        )
        outcome.append(jnp.where(allowed[:, None, :], raw_scores, MASKED))
    return outcome


def head_peaks(score_list):
    return jnp.stack([jnp.max(scores, axis=2) for scores in score_list], axis=1)


def head_sums(score_list, row_shift, key_rows, allowed):
    kv_width = key_rows.shape[1] // 2
    head_dim = kv_width // len(score_list)
    numerators = []
    totals = []
    for head_no, scores in enumerate(score_list):
        weights = jnp.where(
            allowed[:, None, :], jnp.exp(scores - row_shift[:, head_no, :, None]), 0.0
        )
        value_part = key_rows[
            :, kv_width + head_no * head_dim : kv_width + (head_no + 1) * head_dim
        ]
        numerators.append(
            jnp.einsum(
                "ngp,pd->ngd",
                weights.astype(jnp.bfloat16),
                value_part,
                preferred_element_type=jnp.float32,
            )
        )
        totals.append(jnp.sum(weights, axis=2))
    return (jnp.stack(numerators, axis=1), jnp.stack(totals, axis=1))


def join_parts(pre_peak, pre_num, pre_total, self_peak, self_num, self_total):
    row_top = jnp.maximum(pre_peak, self_peak)
    pre_factor = jnp.exp(pre_peak - row_top)
    self_factor = jnp.exp(self_peak - row_top)
    combined = pre_num * pre_factor[..., None] + self_num * self_factor[..., None]
    divisor = pre_total * pre_factor + self_total * self_factor
    return combined / divisor[..., None]


def fold_rows(source, pieces):
    return tuple(
        (jnp.dot(source, piece_now, preferred_element_type=jnp.float32) for piece_now in pieces)
    )


def per_device(
    hidden,
    norm_gains,
    head_gains,
    query_weight,
    kv_weight,
    out_weight,
    gate_up,
    down_weight,
    next_weight,
    expert_ids,
    route_weights,
    token_request,
    request_leaf,
    leaf_parent,
    mid_parent,
    root_length,
    mid_length,
    leaf_length,
    root_slot,
    mid_slot,
    leaf_slot,
    root_cache,
    mid_cache,
    leaf_cache,
):
    tok_rows = hidden.shape[0]
    model_dim = hidden.shape[1]
    head_dim = head_gains.shape[1]
    kv_width = kv_weight.shape[1] // 2
    kv_heads = kv_width // head_dim
    query_width = query_weight.shape[1]
    head_count = query_width // head_dim
    head_ratio = head_count // kv_heads
    group_tok = token_request.shape[0]
    mp_size = lax.axis_size("mp")
    devices_all = lax.axis_size("dp") * mp_size
    my_first = lax.axis_index("mp") * tok_rows
    lengths = (root_length, mid_length, leaf_length)
    slot_tables = (root_slot, mid_slot, leaf_slot)
    my_request = lax.dynamic_slice_in_dim(token_request, my_first, tok_rows)
    request_first = jnp.sum(
        (token_request[None, :] < my_request[:, None]).astype(jnp.int32), axis=1
    )
    my_places = my_first + jnp.arange(tok_rows, dtype=jnp.int32)
    my_slots, my_lengths = tree_paths(
        my_request, request_leaf, leaf_parent, mid_parent, lengths, slot_tables
    )
    positions = my_lengths[0] + my_lengths[1] + my_lengths[2] + my_places - request_first
    normed = rms_norm(hidden, norm_gains[0]).astype(jnp.bfloat16)
    query_raw, kv_raw = fold_rows(
        normed,
        (
            lax.all_gather(query_weight, ("dp", "mp"), axis=0, tiled=True),
            lax.all_gather(kv_weight, ("dp", "mp"), axis=0, tiled=True),
        ),
    )
    queries = rotate(
        rms_norm(query_raw.reshape(tok_rows, head_count, head_dim), head_gains[0]), positions
    ).astype(jnp.bfloat16)
    new_keys = rotate(
        rms_norm(kv_raw[:, :kv_width].reshape(tok_rows, kv_heads, head_dim), head_gains[1]),
        positions,
    ).astype(jnp.bfloat16)
    new_rows = jnp.concatenate(
        [new_keys.reshape(tok_rows, kv_width), kv_raw[:, kv_width:].astype(jnp.bfloat16)], axis=1
    )
    group_rows = lax.all_gather(new_rows, "mp", axis=0, tiled=True)
    self_allowed = (my_request[:, None] == token_request[None, :]) & (
        jnp.arange(group_tok, dtype=jnp.int32)[None, :] <= my_places[:, None]
    )
    my_queries = queries.reshape(tok_rows, kv_heads, head_ratio, head_dim)
    self_scores = head_scores(my_queries, group_rows, self_allowed)
    self_peak = head_peaks(self_scores)
    self_num, self_total = head_sums(self_scores, self_peak, group_rows, self_allowed)
    gathered = (
        lax.all_gather(root_cache, "mp", axis=0, tiled=True),
        lax.all_gather(mid_cache, "mp", axis=0, tiled=True),
        lax.all_gather(leaf_cache, "mp", axis=0, tiled=True),
    )
    first_request = token_request[0]
    path_rows = []
    path_masks = []
    for request_no in range(REQ_GRP):
        request_id = first_request + request_no
        chosen_slots, chosen_lengths = tree_paths(
            jnp.reshape(request_id, (1,)),
            request_leaf,
            leaf_parent,
            mid_parent,
            lengths,
            slot_tables,
        )
        mine = my_request == request_id
        for level_no in range(3):
            level_part = gathered[level_no]
            path_rows.append(
                lax.dynamic_index_in_dim(level_part, chosen_slots[level_no][0], 0, keepdims=False)
            )
            within = jnp.arange(level_part.shape[1], dtype=jnp.int32)
            path_masks.append(mine[:, None] & (within[None, :] < chosen_lengths[level_no][0]))
    prefix_rows = jnp.concatenate(path_rows, axis=0)
    prefix_allowed = jnp.concatenate(path_masks, axis=1)
    pre_scores = head_scores(my_queries, prefix_rows, prefix_allowed)
    pre_peak = head_peaks(pre_scores)
    pre_num, pre_total = head_sums(pre_scores, pre_peak, prefix_rows, prefix_allowed)
    attended = (
        join_parts(pre_peak, pre_num, pre_total, self_peak, self_num, self_total)
        .reshape(tok_rows, query_width)
        .astype(jnp.bfloat16)
    )
    projected = fold_rows(
        attended, (lax.all_gather(out_weight, ("dp", "mp"), axis=0, tiled=True),)
    )[0]
    after_attention = (hidden.astype(jnp.float32) + projected).astype(jnp.bfloat16)
    moe_in = rms_norm(after_attention, norm_gains[1]).astype(jnp.bfloat16)
    top_k = expert_ids.shape[1]
    experts_all = gate_up.shape[0] * devices_all
    capacity = max(2, 5 * tok_rows * top_k // (4 * experts_all))
    flat_ids = expert_ids.reshape(-1)
    flat_count = flat_ids.shape[0]
    order_ids = jnp.arange(flat_count, dtype=jnp.int32)
    earlier = (flat_ids[:, None] == flat_ids[None, :]) & (order_ids[None, :] < order_ids[:, None])
    slot_no = jnp.sum(earlier.astype(jnp.int32), axis=1)
    target = flat_ids * capacity + slot_no
    spread_rows = jnp.broadcast_to(moe_in[:, None, :], (tok_rows, top_k, model_dim)).reshape(
        flat_count, model_dim
    )
    outbound = (
        jnp.zeros((experts_all * capacity, model_dim), jnp.bfloat16).at[target].set(spread_rows)
    )
    block_in = lax.all_to_all(
        outbound.reshape(devices_all, 1, capacity, model_dim),
        ("dp", "mp"),
        split_axis=0,
        concat_axis=1,
        tiled=True,
    )
    rows_in = block_in.reshape(-1, model_dim)
    gate_up_out = jnp.dot(rows_in, gate_up[0], preferred_element_type=jnp.float32)
    ff_width = down_weight.shape[1]
    active = (jax.nn.silu(gate_up_out[:, :ff_width]) * gate_up_out[:, ff_width:]).astype(
        jnp.bfloat16
    )
    served = (
        jnp.dot(active, down_weight[0], preferred_element_type=jnp.float32)
        .astype(jnp.bfloat16)
        .reshape(block_in.shape)
    )
    returned = lax.all_to_all(served, ("dp", "mp"), split_axis=1, concat_axis=0, tiled=True)
    expert_rows = returned.reshape(experts_all * capacity, model_dim)[target]
    mixture = jnp.sum(
        expert_rows.astype(jnp.float32).reshape(tok_rows, top_k, model_dim)
        * route_weights[:, :, None],
        axis=1,
    )
    layer_out = (after_attention.astype(jnp.float32) + mixture).astype(jnp.bfloat16)
    next_in = rms_norm(layer_out, norm_gains[2]).astype(jnp.bfloat16)
    next_raw = fold_rows(next_in, (lax.all_gather(next_weight, ("dp", "mp"), axis=0, tiled=True),))[
        0
    ]
    next_keys = rotate(
        rms_norm(next_raw[:, :kv_width].reshape(tok_rows, kv_heads, head_dim), head_gains[2]),
        positions,
    ).astype(jnp.bfloat16)
    next_rows = jnp.concatenate(
        [next_keys.reshape(tok_rows, kv_width), next_raw[:, kv_width:].astype(jnp.bfloat16)], axis=1
    )
    return (layer_out, next_rows)


def solution(mesh):
    placed = (
        P(("dp", "mp"), None),
        P(),
        P(),
        P(("dp", "mp"), None),
        P(("dp", "mp"), None),
        P(("dp", "mp"), None),
        P(("dp", "mp"), None, None),
        P(("dp", "mp"), None, None),
        P(("dp", "mp"), None),
        P(("dp", "mp"), None),
        P(("dp", "mp"), None),
        P("dp"),
        P(),
        P(),
        P(),
        P(),
        P(),
        P(),
        P(),
        P(),
        P(),
        P("mp", None, None),
        P("mp", None, None),
        P("mp", None, None),
    )
    return jax.shard_map(
        per_device,
        mesh=mesh,
        in_specs=placed,
        out_specs=(P(("dp", "mp"), None), P(("dp", "mp"), None)),
        check_vma=False,
    )
```

profile of v0, /device:TPU:9, one launch (start us, length us, event | category | flops | bytes accessed | tf_op | source)
XLA Modules:
  0.0 1670.7 jit_solution(7209893921031694401)
XLA Ops:
  22.1 290.2 %all-gather.17.cloned.1.call-done = bf16[2048,512]{1,0:T(8,128)(2,1)} async-done(((bf16[16,512]{1,0:T(8,128)(2,1)}), bf16[2048,512]{1,0:T(8,128)(2,1)}) %all-gather.17.cloned.1.call-update) | async-done | bytes 2097168 | tf_op jit(solution)/shard_map/all_gather | solution.py:164
  337.0 2.7 select_reduce_fusion.6
  356.5 10.2 all-gather.11.cloned.1.call-done
  368.7 34.8 %all-gather.13.cloned.1.call-done = bf16[8,256,512]{2,1,0:T(8,128)(2,1)} async-done(((bf16[1,256,512]{2,1,0:T(8,128)(2,1)}), bf16[8,256,512]{2,1,0:T(8,128)(2,1)}) %all-gather.13.cloned.1.call-update) | async-done | bytes 2097168 | tf_op jit(solution)/shard_map/all_gather | solution.py:187
  405.2 40.7 %all-gather.15.cloned.1.call-done = bf16[16,128,512]{2,1,0:T(8,128)(2,1)} async-done(((bf16[2,128,512]{2,1,0:T(8,128)(2,1)}), bf16[16,128,512]{2,1,0:T(8,128)(2,1)}) %all-gather.15.cloned.1.call-update) | async-done | bytes 2097168 | tf_op jit(solution)/shard_map/all_gather | solution.py:188
  452.5 312.0 %all-gather.9.cloned.1.call-done = bf16[2048,2048]{1,0:T(8,128)(2,1)} async-done(((bf16[16,2048]{1,0:T(8,128)(2,1)}), bf16[2048,2048]{1,0:T(8,128)(2,1)}) %all-gather.9.cloned.1.call-update) | async-done | bytes 8388624 | tf_op jit(solution)/shard_map/all_gather | solution.py:163
  764.5 4.9 convolution_bitcast_fusion
  778.1 22.6 %all-gather.19.cloned.1.call-done = bf16[1024,512]{1,0:T(8,128)(2,1)} async-done(((bf16[128,512]{1,0:T(8,128)(2,1)}), bf16[1024,512]{1,0:T(8,128)(2,1)}) %all-gather.19.cloned.1.call-update) | async-done | bytes 1048592 | tf_op jit(solution)/shard_map/all_gather | solution.py:177
  808.3 3.7 fusion.5
  822.0 296.9 %all-gather.21.cloned.1.call-done = bf16[2048,2048]{1,0:T(8,128)(2,1)} async-done(((bf16[16,2048]{1,0:T(8,128)(2,1)}), bf16[2048,2048]{1,0:T(8,128)(2,1)}) %all-gather.21.cloned.1.call-update) | async-done | bytes 8388624 | tf_op jit(solution)/shard_map/all_gather | solution.py:222
  1119.0 4.9 multiply_reduce_fusion
  1125.9 10.4 scatter_custom_fusion
  1136.2 9.5 reshape.559
  1145.7 104.9 %all_to_all.8 = bf16[128,1,10,2048]{3,2,1,0:T(8,128)(2,1)} all-to-all(bf16[128,1,10,2048]{3,2,1,0:T(8,128)(2,1)} %bitcast.122), channel_id=1, replica_groups=mesh['dp'=16,'mp'=8] {'dp','mp'}, dimensions={0} | all-to-all | bytes 10485760 | tf_op jit(solution)/shard_map/all_to_all | solution.py:241
  1250.7 9.8 reshape.560
  1260.5 12.1 fusion.3
  1272.6 6.1 convolution_convert_fusion
  1278.7 9.5 reshape.561
  1288.2 8.8 all-to-all-start.1
  1297.8 104.0 %all-to-all-done.1 = bf16[1,128,10,2048]{3,2,0,1:T(8,128)(2,1)} async-done(((bf16[1,128,10,2048]{3,2,0,1:T(8,128)(2,1)}), bf16[1,128,10,2048]{3,2,0,1:T(8,128)(2,1)}, u32[]{:S(2)}, u32[]{:S(2)}) %all-to-all-start.1) | async-done | bytes 5242912 | tf_op jit(solution)/shard_map/all_to_all | solution.py:259
  1401.9 9.8 reshape.562
  1411.7 12.0 gather_fusion
  1423.7 6.6 fusion
  1431.3 226.8 %all-gather.23.cloned.1.call-done = bf16[2048,512]{1,0:T(8,128)(2,1)} async-done(((bf16[16,512]{1,0:T(8,128)(2,1)}), bf16[2048,512]{1,0:T(8,128)(2,1)}) %all-gather.23.cloned.1.call-update) | async-done | bytes 2097168 | tf_op jit(solution)/shard_map/all_gather | solution.py:268
  (156 shorter events, 89.9 us)
Async XLA Ops:
  7.2 1265.4 %copy-start = (bf16[1,768,2048]{2,1,0:T(8,128)(2,1)S(1)}, bf16[1,768,2048]{2,1,0:T(8,128)(2,1)}, u32[]{:S(2)}) copy-start(bf16[1,768,2048]{2,1,0:T(8,128)(2,1)} %param.31) | copy-start | bytes 9437188
  7.2 305.2 %all-gather.17.cloned.1.call-start = ((), (), s32[]{:S(2)}) async-start(), calls=%async_computation.6 | async-start | bytes 2113536 | tf_op jit(solution)/shard_map/all_gather | solution.py:164
  7.9 358.8 %all-gather.11.cloned.1.call-start = ((), (), s32[]{:S(2)}) async-start(), calls=%async_computation.3 | async-start | bytes 4718592 | tf_op jit(solution)/shard_map/all_gather | solution.py:186
  8.7 394.8 %all-gather.13.cloned.1.call-start = ((), (), s32[]{:S(2)}) async-start(), calls=%async_computation.4 | async-start | bytes 2359296 | tf_op jit(solution)/shard_map/all_gather | solution.py:187
  9.4 436.4 %all-gather.15.cloned.1.call-start = ((), (), s32[]{:S(2)}) async-start(), calls=%async_computation.5 | async-start | bytes 2359296 | tf_op jit(solution)/shard_map/all_gather | solution.py:188
  10.0 754.5 %all-gather.9.cloned.1.call-start = ((), (), s32[]{:S(2)}) async-start(), calls=%async_computation.2 | async-start | bytes 8454144 | tf_op jit(solution)/shard_map/all_gather | solution.py:163
  10.6 790.2 %all-gather.19.cloned.1.call-start = ((), (), s32[]{:S(2)}) async-start(), calls=%async_computation.7 | async-start | bytes 1179648 | tf_op jit(solution)/shard_map/all_gather | solution.py:177
  13.7 3.0 copy-start.18
  18.9 296.4 %copy-start.16 = (f32[128]{0:T(128)}, f32[128]{0:T(128)S(1)}, u32[]{:S(2)}) copy-start(f32[128]{0:T(128)S(1)} %add_rsqrt_fusion.5) | copy-start | bytes 1540
  20.6 332.6 %copy-start.8 = (f32[128,64]{1,0:T(8,128)}, f32[128,64]{1,0:T(8,128)S(1)}, u32[]{:S(2)}) copy-start(f32[128,64]{1,0:T(8,128)S(1)} %get-tuple-element.47) | copy-start | bytes 98308
  20.6 332.6 %copy-start.10 = (f32[128,64]{1,0:T(8,128)}, f32[128,64]{1,0:T(8,128)S(1)}, u32[]{:S(2)}) copy-start(f32[128,64]{1,0:T(8,128)S(1)} %get-tuple-element.48) | copy-start | bytes 98308
  315.3 449.2 %copy-start.17 = (f32[128]{0:T(128)S(1)}, f32[128]{0:T(128)}, u32[]{:S(2)}) copy-start(f32[128]{0:T(128)} %copy-done.16) | copy-start | bytes 1540
  318.5 800.5 %all-gather.21.cloned.1.call-start = ((), (), s32[]{:S(2)}) async-start(), calls=%async_computation.8 | async-start | bytes 8454144 | tf_op jit(solution)/shard_map/all_gather | solution.py:222
  452.5 320.7 %copy-start.21 = (f32[128]{0:T(128)S(1)}, f32[128]{0:T(128)}, u32[]{:S(2)}) copy-start(f32[128]{0:T(128)} %get-tuple-element.45) | copy-start | bytes 1540
  800.7 2.3 copy-start.7
  800.7 2.3 copy-start.12
  1119.0 5.9 copy-start.15
  1288.2 9.5 copy-start.19
  1288.2 113.7 %all-to-all-start.1 = ((bf16[1,128,10,2048]{3,2,0,1:T(8,128)(2,1)}), bf16[1,128,10,2048]{3,2,0,1:T(8,128)(2,1)}, u32[]{:S(2)}, u32[]{:S(2)}) async-start(bf16[1,128,10,2048]{3,2,0,1:T(8,128)(2,1)} %bitcast.121), calls=%async_computation.1 | async-start | bytes 16777216 | tf_op jit(solution)/shard_map/all_to_all | solution.py:259
  1297.0 361.1 %all-gather.23.cloned.1.call-start = ((), (), s32[]{:S(2)}) async-start(), calls=%async_computation.9 | async-start | bytes 2113536 | tf_op jit(solution)/shard_map/all_gather | solution.py:268
  1423.7 6.6 copy-start.2
  1430.3 231.0 %copy-start.20 = (f32[128]{0:T(128)S(1)}, f32[128]{0:T(128)}, u32[]{:S(2)}) copy-start(f32[128]{0:T(128)} %get-tuple-element.44) | copy-start | bytes 1540
  1430.3 231.2 %copy-start.9 = (f32[128,64]{1,0:T(8,128)S(1)}, f32[128,64]{1,0:T(8,128)}, u32[]{:S(2)}) copy-start(f32[128,64]{1,0:T(8,128)} %copy-done.8) | copy-start | bytes 98308
  1430.3 231.2 %copy-start.11 = (f32[128,64]{1,0:T(8,128)S(1)}, f32[128,64]{1,0:T(8,128)}, u32[]{:S(2)}) copy-start(f32[128,64]{1,0:T(8,128)} %copy-done.10) | copy-start | bytes 98308
  (7 other events, 9.1 us)
Sparse Core Ops, SparseCore 0:
  9.7 302.5 all-gather.16
  314.0 52.7 all-gather.10
  368.4 35.0 all-gather.12
  405.0 40.8 all-gather.14
  447.4 317.0 all-gather.8
  766.6 34.1 all-gather.18
  802.4 316.5 all-gather.20
  1299.5 358.5 all-gather.22
where the time goes:
time: 1680 us; the launch traced here: 1670 us
  waiting for transfers between devices  1340 us (80%)
  blocking collectives  105 us (6%)
  local copies, waits for them, and re-layouts  83 us (5%)
  other arithmetic  55.1 us (3%)
  matrix products  49 us (3%)
  between operations  26.7 us (2%)
    all_gather x1, waiting for transfers between devices, per_device(): lax.all_gather(query_weight, ('dp', 'mp'), axis=0, tiled=True)  312 us
    all_gather x1, waiting for transfers between devices, per_device(): lax.all_gather(out_weight, ('dp', 'mp'), axis=0, tiled=True)  297 us
    all_gather x1, waiting for transfers between devices, per_device(): lax.all_gather(kv_weight, ('dp', 'mp'), axis=0, tiled=True)  290 us
    all_gather x1, waiting for transfers between devices, per_device(): lax.all_gather(next_weight, ('dp', 'mp'), axis=0, tiled=True)  227 us
    all_to_all x1, blocking collectives, per_device(): lax.all_to_all(outbound.reshape(devices_all, 1, capacity, model_dim), ('d...  105 us
    all_to_all x1, waiting for transfers between devices, per_device(): lax.all_to_all(served, ('dp', 'mp'), split_axis=1, concat_axis=0, tiled=T...  104 us
    all_gather x1, waiting for transfers between devices, per_device(): lax.all_gather(leaf_cache, 'mp', axis=0, tiled=True)  40.7 us
    all_gather x1, waiting for transfers between devices, per_device(): lax.all_gather(mid_cache, 'mp', axis=0, tiled=True)  34.8 us
  transfers between devices with their start and end apart: 9, of which 9 were waited for; matrix products, arithmetic and copies ran while one was open for 7% of the time, Pallas kernels for 0%

commit v1 on v0

--- a/solution.py
+++ b/solution.py
@@ -256,7 +256,9 @@
         .astype(jnp.bfloat16)
         .reshape(block_in.shape)
     )
-    returned = lax.all_to_all(served, ("dp", "mp"), split_axis=1, concat_axis=0, tiled=True)
+    parts = jnp.split(served, lax.axis_size(("dp", "mp")), axis=1)
+    received = lax.all_to_all(jnp.stack(parts), ("dp", "mp"), 0, 0)
+    returned = jnp.concatenate(received, axis=0)
     expert_rows = returned.reshape(experts_all * capacity, model_dim)[target]
     mixture = jnp.sum(
         expert_rows.astype(jnp.float32).reshape(tok_rows, top_k, model_dim)

time: 1680 us -> 1870 us (1.11)
  local copies, waits for them, and re-layouts: 83 us -> 270 us
    unnamed x54 -> x173, local copies, waits for them, and re-layouts: 12.7 us -> 198 us
  transfers between devices with their start and end apart: 9 -> 9, of which waited for: 9 -> 9; matrix products, arithmetic and copies ran while one was open for 7% -> 6% of each run, Pallas kernels for 0% -> 0%
where the time goes in v1:
time: 1870 us; the launch traced here: 1860 us
  waiting for transfers between devices  1340 us (72%)
  local copies, waits for them, and re-layouts  270 us (14%)
  blocking collectives  104 us (6%)
  other arithmetic  56.3 us (3%)
  matrix products  50.2 us (3%)
  between operations  27 us (1%)
    all_gather x1, waiting for transfers between devices, per_device(): lax.all_gather(query_weight, ('dp', 'mp'), axis=0, tiled=True)  312 us
    all_gather x1, waiting for transfers between devices, per_device(): lax.all_gather(out_weight, ('dp', 'mp'), axis=0, tiled=True)  295 us
    all_gather x1, waiting for transfers between devices, per_device(): lax.all_gather(kv_weight, ('dp', 'mp'), axis=0, tiled=True)  290 us
    all_gather x1, waiting for transfers between devices, per_device(): lax.all_gather(next_weight, ('dp', 'mp'), axis=0, tiled=True)  227 us
    unnamed x173, local copies, waits for them, and re-layouts  198 us
    all_to_all x1, blocking collectives, per_device(): lax.all_to_all(outbound.reshape(devices_all, 1, capacity, model_dim), ('d...  104 us
    all_to_all x1, waiting for transfers between devices, per_device(): received = lax.all_to_all(jnp.stack(parts), ('dp', 'mp'), 0, 0)  104 us
    all_gather x1, waiting for transfers between devices, per_device(): lax.all_gather(leaf_cache, 'mp', axis=0, tiled=True)  40.7 us
  transfers between devices with their start and end apart: 9, of which 9 were waited for; matrix products, arithmetic and copies ran while one was open for 6% of the time, Pallas kernels for 0%

profile of v1, /device:TPU:9, one launch (start us, length us, event | category | flops | bytes accessed | tf_op | source)
XLA Modules:
  0.0 1858.0 jit_solution(10648028748578931182)
XLA Ops:
  22.1 290.2 %all-gather.17.cloned.1.call-done = bf16[2048,512]{1,0:T(8,128)(2,1)} async-done(((bf16[16,512]{1,0:T(8,128)(2,1)}), bf16[2048,512]{1,0:T(8,128)(2,1)}) %all-gather.17.cloned.1.call-update) | async-done | bytes 2097168 | tf_op jit(solution)/shard_map/all_gather | solution.py:164
  356.5 10.2 all-gather.11.cloned.1.call-done
  368.7 34.8 %all-gather.13.cloned.1.call-done = bf16[8,256,512]{2,1,0:T(8,128)(2,1)} async-done(((bf16[1,256,512]{2,1,0:T(8,128)(2,1)}), bf16[8,256,512]{2,1,0:T(8,128)(2,1)}) %all-gather.13.cloned.1.call-update) | async-done | bytes 2097168 | tf_op jit(solution)/shard_map/all_gather | solution.py:187
  405.2 40.7 %all-gather.15.cloned.1.call-done = bf16[16,128,512]{2,1,0:T(8,128)(2,1)} async-done(((bf16[2,128,512]{2,1,0:T(8,128)(2,1)}), bf16[16,128,512]{2,1,0:T(8,128)(2,1)}) %all-gather.15.cloned.1.call-update) | async-done | bytes 2097168 | tf_op jit(solution)/shard_map/all_gather | solution.py:188
  452.5 312.0 %all-gather.9.cloned.1.call-done = bf16[2048,2048]{1,0:T(8,128)(2,1)} async-done(((bf16[16,2048]{1,0:T(8,128)(2,1)}), bf16[2048,2048]{1,0:T(8,128)(2,1)}) %all-gather.9.cloned.1.call-update) | async-done | bytes 8388624 | tf_op jit(solution)/shard_map/all_gather | solution.py:163
  764.5 4.9 convolution_bitcast_fusion
  778.1 22.6 %all-gather.19.cloned.1.call-done = bf16[1024,512]{1,0:T(8,128)(2,1)} async-done(((bf16[128,512]{1,0:T(8,128)(2,1)}), bf16[1024,512]{1,0:T(8,128)(2,1)}) %all-gather.19.cloned.1.call-update) | async-done | bytes 1048592 | tf_op jit(solution)/shard_map/all_gather | solution.py:177
  803.0 2.8 fusion.1
  809.4 3.7 fusion.5
  823.1 295.5 %all-gather.21.cloned.1.call-done = bf16[2048,2048]{1,0:T(8,128)(2,1)} async-done(((bf16[16,2048]{1,0:T(8,128)(2,1)}), bf16[2048,2048]{1,0:T(8,128)(2,1)}) %all-gather.21.cloned.1.call-update) | async-done | bytes 8388624 | tf_op jit(solution)/shard_map/all_gather | solution.py:222
  1118.6 4.9 multiply_reduce_fusion
  1125.5 10.4 scatter_custom_fusion
  1135.9 9.5 reshape.552
  1145.4 104.4 %all_to_all.14 = bf16[128,1,10,2048]{3,2,1,0:T(8,128)(2,1)} all-to-all(bf16[128,1,10,2048]{3,2,1,0:T(8,128)(2,1)} %bitcast.630), channel_id=1, replica_groups=mesh['dp'=16,'mp'=8] {'dp','mp'}, dimensions={0} | all-to-all | bytes 10485760 | tf_op jit(solution)/shard_map/all_to_all | solution.py:241
  1249.8 9.8 reshape.553
  1259.6 12.1 fusion.3
  1271.7 6.1 convolution_convert_fusion
  1277.8 9.5 reshape.554
  1474.4 8.6 all-to-all-start.1
  1483.8 104.0 %all-to-all-done.1 = bf16[128,1,1,10,2048]{4,3,2,1,0:T(8,128)(2,1)} async-done(((bf16[128,1,1,10,2048]{4,3,2,1,0:T(8,128)(2,1)}), bf16[128,1,1,10,2048]{4,3,2,1,0:T(8,128)(2,1)}, u32[]{:S(2)}, u32[]{:S(2)}) %all-to-all-start.1) | async-done | bytes 5242912 | tf_op jit(solution)/shard_map/all_to_all | solution.py:260
  1587.8 10.1 reshape_reshape.3
  1597.9 12.0 gather_fusion
  1610.0 6.5 fusion
  1618.7 226.5 %all-gather.23.cloned.1.call-done = bf16[2048,512]{1,0:T(8,128)(2,1)} async-done(((bf16[16,512]{1,0:T(8,128)(2,1)}), bf16[2048,512]{1,0:T(8,128)(2,1)}) %all-gather.23.cloned.1.call-update) | async-done | bytes 2097168 | tf_op jit(solution)/shard_map/all_gather | solution.py:270
  (276 shorter events, 279.2 us)
Async XLA Ops:
  7.2 1264.5 %copy-start = (bf16[1,768,2048]{2,1,0:T(8,128)(2,1)S(1)}, bf16[1,768,2048]{2,1,0:T(8,128)(2,1)}, u32[]{:S(2)}) copy-start(bf16[1,768,2048]{2,1,0:T(8,128)(2,1)} %param.31) | copy-start | bytes 9437188
  7.2 305.2 %all-gather.17.cloned.1.call-start = ((), (), s32[]{:S(2)}) async-start(), calls=%async_computation.6 | async-start | bytes 2113536 | tf_op jit(solution)/shard_map/all_gather | solution.py:164
  7.9 358.8 %all-gather.11.cloned.1.call-start = ((), (), s32[]{:S(2)}) async-start(), calls=%async_computation.3 | async-start | bytes 4718592 | tf_op jit(solution)/shard_map/all_gather | solution.py:186
  8.7 394.8 %all-gather.13.cloned.1.call-start = ((), (), s32[]{:S(2)}) async-start(), calls=%async_computation.4 | async-start | bytes 2359296 | tf_op jit(solution)/shard_map/all_gather | solution.py:187
  9.4 436.4 %all-gather.15.cloned.1.call-start = ((), (), s32[]{:S(2)}) async-start(), calls=%async_computation.5 | async-start | bytes 2359296 | tf_op jit(solution)/shard_map/all_gather | solution.py:188
  10.0 754.5 %all-gather.9.cloned.1.call-start = ((), (), s32[]{:S(2)}) async-start(), calls=%async_computation.2 | async-start | bytes 8454144 | tf_op jit(solution)/shard_map/all_gather | solution.py:163
  10.6 790.2 %all-gather.19.cloned.1.call-start = ((), (), s32[]{:S(2)}) async-start(), calls=%async_computation.7 | async-start | bytes 1179648 | tf_op jit(solution)/shard_map/all_gather | solution.py:177
  13.7 3.0 copy-start.14
  18.9 296.4 %copy-start.13 = (f32[128]{0:T(128)}, f32[128]{0:T(128)S(1)}, u32[]{:S(2)}) copy-start(f32[128]{0:T(128)S(1)} %add_rsqrt_fusion.5) | copy-start | bytes 1540
  20.6 332.6 %copy-start.5 = (f32[128,64]{1,0:T(8,128)}, f32[128,64]{1,0:T(8,128)S(1)}, u32[]{:S(2)}) copy-start(f32[128,64]{1,0:T(8,128)S(1)} %get-tuple-element.47) | copy-start | bytes 98308
  20.6 332.6 %copy-start.7 = (f32[128,64]{1,0:T(8,128)}, f32[128,64]{1,0:T(8,128)S(1)}, u32[]{:S(2)}) copy-start(f32[128,64]{1,0:T(8,128)S(1)} %get-tuple-element.48) | copy-start | bytes 98308
  318.5 800.2 %all-gather.21.cloned.1.call-start = ((), (), s32[]{:S(2)}) async-start(), calls=%async_computation.8 | async-start | bytes 8454144 | tf_op jit(solution)/shard_map/all_gather | solution.py:222
  452.5 320.7 %copy-start.17 = (f32[128]{0:T(128)S(1)}, f32[128]{0:T(128)}, u32[]{:S(2)}) copy-start(f32[128]{0:T(128)} %get-tuple-element.45) | copy-start | bytes 1540
  800.7 5.0 copy-start.10
  800.7 5.0 copy-start.11
  805.8 3.6 copy-start.9
  1118.6 5.9 copy-start.12
  1123.6 1.0 copy-start.1
  1474.4 9.3 copy-start.15
  1474.4 113.5 %all-to-all-start.1 = ((bf16[128,1,1,10,2048]{4,3,2,1,0:T(8,128)(2,1)}), bf16[128,1,1,10,2048]{4,3,2,1,0:T(8,128)(2,1)}, u32[]{:S(2)}, u32[]{:S(2)}) async-start(bf16[128,1,1,10,2048]{4,3,2,1,0:T(8,128)(2,1)} %constant_dynamic-update-slice_fusion.10), calls=%async_computation.1 | async-start | bytes 16777216 | tf_op jit(solution)/shard_map/all_to_all | solution.py:260
  1482.9 362.3 %all-gather.23.cloned.1.call-start = ((), (), s32[]{:S(2)}) async-start(), calls=%async_computation.9 | async-start | bytes 2113536 | tf_op jit(solution)/shard_map/all_gather | solution.py:270
  1609.9 238.5 %copy-start.16 = (f32[128]{0:T(128)S(1)}, f32[128]{0:T(128)}, u32[]{:S(2)}) copy-start(f32[128]{0:T(128)} %get-tuple-element.44) | copy-start | bytes 1540
  1610.0 238.7 %copy-start.6 = (f32[128,64]{1,0:T(8,128)S(1)}, f32[128,64]{1,0:T(8,128)}, u32[]{:S(2)}) copy-start(f32[128,64]{1,0:T(8,128)} %copy-done.5) | copy-start | bytes 98308
  1610.0 238.7 %copy-start.8 = (f32[128,64]{1,0:T(8,128)S(1)}, f32[128,64]{1,0:T(8,128)}, u32[]{:S(2)}) copy-start(f32[128,64]{1,0:T(8,128)} %copy-done.7) | copy-start | bytes 98308
  (3 other events, 2.6 us)
Sparse Core Ops, SparseCore 0:
  9.7 302.5 all-gather.16
  314.0 52.7 all-gather.10
  368.4 35.0 all-gather.12
  405.0 40.8 all-gather.14
  447.4 317.0 all-gather.8
  766.6 34.1 all-gather.18
  802.4 316.1 all-gather.20
  1485.5 359.7 all-gather.22
